TPU v7x, 32 devices: a whole 2x2x4 slice. The times are simulated.
32 devices in a mesh: dp: 4 (over x, core), fsdp: 8 (over z, y).
Axes of the slice: x: 2, y: 2, z: 4, core: 2. Of those that a mesh axis runs over, the one named last changes fastest.
Arguments:
- token_ids: int32 [4096], P('dp'), may hold values from 0 to 15263, as said below
- embed_table: bfloat16 [15264, 768], P('fsdp'), may hold values from -16 to 16, as said below
- w_qkv: bfloat16 [768, 2304], P('fsdp'), may hold values from -2 to 2
- w_out: bfloat16 [768, 768], P('fsdp'), may hold values from -0.21875 to 0.21875
- ln_gain: float32 [768], replicated, may hold values from 0.5 to 1.5
- ln_bias: float32 [768], replicated, may hold values from -1 to 1
- centroids_t: bfloat16 [768, 32768], P('fsdp', 'dp'), may hold values from -24 to 24
- assignments: int32 [4096], replicated, may hold values from 0 to 32767, as said below
Outputs:
- token_loss: float32 [4096], P(('dp', 'fsdp'))
- new_centroids: float32 [32768, 768], P(('dp', 'fsdp'))
Inputs may be any that keep to these rules, and one draw needn't show every extreme that they name: `token_ids`: id 0 is padding; a passage may end in a run of padding. `embed_table`: token embeddings of order one. `assignments`: cluster sizes are skewed.
All inputs are finite; a program needn't handle non-finite values.
Results may differ from a plain program's by a relative error of at most 0.0055.
Values may be sent and summed in bfloat16 or wider, within the bound.
A program may use at most 64 MiB of HBM per device.

v0:
```python
import math

import jax
import jax.numpy as jnp
from jax import lax
from jax.sharding import PartitionSpec as P

HEADS = 12
HEAD = 64
SEQ = 128


def joined(shard, axis, combine):
    everything = jax.tree.map(lambda part: lax.all_gather(part, axis), shard)
    initial = jax.tree.map(lambda part: part[0], everything)

    def lap(k, so_far):
        return combine(so_far, jax.tree.map(lambda part: part[k], everything))

    return lax.fori_loop(1, lax.axis_size(axis), lap, initial)


def layer_norm(values, ln_gain, ln_bias):
    center = values - jnp.mean(values, axis=-1, keepdims=True)
    spread = jnp.mean(center * center, axis=-1, keepdims=True)
    return center * lax.rsqrt(spread + 1e-05) * ln_gain + ln_bias


def encode(inputs, qkv_full, out_full, ln_gain, ln_bias):
    passages = inputs.shape[0] // SEQ
    packed = jnp.dot(inputs, qkv_full, preferred_element_type=jnp.float32).astype(jnp.bfloat16)
    packed = packed.reshape(passages, SEQ, 3, HEADS, HEAD)
    scores = jnp.einsum(
        "bqhd,bkhd->bhqk", packed[:, :, 0], packed[:, :, 1], preferred_element_type=jnp.float32
    ) * (1.0 / math.sqrt(HEAD))
    probs = jax.nn.softmax(scores, axis=-1).astype(jnp.bfloat16)
    context = jnp.einsum(
        "bhqk,bkhd->bqhd", probs, packed[:, :, 2], preferred_element_type=jnp.float32
    )
    context = context.astype(jnp.bfloat16).reshape(inputs.shape[0], HEADS * HEAD)
    mixed = jnp.dot(context, out_full, preferred_element_type=jnp.float32) + inputs.astype(
        jnp.float32
    )
    return layer_norm(mixed, ln_gain, ln_bias).astype(jnp.bfloat16)


def one_hot_sums(rows, targets, width):
    count = rows.shape[0]
    step_rows = math.gcd(count, 512)
    columns = jnp.arange(width, dtype=jnp.int32)

    def one_visit(totals, pieces):
        block_rows, block_targets = pieces
        hits = (block_targets[:, None] == columns[None, :]).astype(jnp.bfloat16)
        return (
            totals
            + lax.dot_general(
                hits, block_rows, (((0,), (0,)), ((), ())), preferred_element_type=jnp.float32
            ),
            None,
        )

    start = jnp.zeros((width, rows.shape[1]), jnp.float32)
    totals, unused = lax.scan(
        one_visit,
        start,
        (
            rows.reshape(count // step_rows, step_rows, rows.shape[1]),
            targets.reshape(count // step_rows, step_rows),
        ),
    )
    return totals


def combine_parts(first, second):
    peak = jnp.maximum(first[0], second[0])
    mass = first[1] * jnp.exp(first[0] - peak) + second[1] * jnp.exp(second[0] - peak)
    return (peak, mass, first[2] + second[2])


def shards(token_ids, embed_table, w_qkv, w_out, ln_gain, ln_bias, centroids_t, assignments):
    dp_size = lax.axis_size("dp")
    fsdp_size = lax.axis_size("fsdp")
    dp_rank = lax.axis_index("dp")
    fsdp_rank = lax.axis_index("fsdp")
    vocab_rows = embed_table.shape[0]
    local_ids = token_ids - fsdp_rank * vocab_rows
    inside = (local_ids >= 0) & (local_ids < vocab_rows)
    looked = jnp.take(embed_table, jnp.clip(local_ids, 0, vocab_rows - 1), axis=0)
    looked = jnp.where(inside[:, None], looked, jnp.zeros_like(looked))
    inputs = (
        lax.psum_scatter(looked, "fsdp", scatter_dimension=0, tiled=True)
        .astype(jnp.float32)
        .astype(jnp.bfloat16)
    )
    qkv_full, out_full, cent_full = (
        lax.all_gather(w_qkv, "fsdp", axis=0, tiled=True),
        lax.all_gather(w_out, "fsdp", axis=0, tiled=True),
        lax.all_gather(centroids_t, "fsdp", axis=0, tiled=True),
    )
    encoded = encode(inputs, qkv_full, out_full, ln_gain, ln_bias)
    own_rows = encoded.shape[0]
    width = encoded.shape[1]
    block_width = cent_full.shape[1]
    per_dev = block_width // fsdp_size
    slab = lax.all_gather(encoded, "dp", axis=0, tiled=True)
    slab_assign = lax.dynamic_index_in_dim(
        assignments.reshape(dp_size, fsdp_size, own_rows), fsdp_rank, 1, keepdims=False
    ).reshape(-1)
    owned = slab_assign - dp_rank * block_width
    slab_rows = slab.shape[0]
    step_rows = math.gcd(slab_rows, 512)
    columns = jnp.arange(block_width, dtype=jnp.int32)

    def body_visit(totals, pieces):
        block_rows, local = pieces
        logits = jnp.dot(block_rows, cent_full, preferred_element_type=jnp.float32)
        peak = jnp.max(logits, axis=1)
        mass = jnp.sum(jnp.exp(logits - peak[:, None]), axis=1)
        hits = local[:, None] == columns[None, :]
        picked = jnp.sum(jnp.where(hits, logits, 0.0), axis=1)
        return (totals, (peak, mass, picked))

    start = jnp.zeros((1,), jnp.float32)
    partial_value, stats = lax.scan(
        body_visit,
        start,
        (
            slab.reshape(slab_rows // step_rows, step_rows, width),
            owned.reshape(slab_rows // step_rows, step_rows),
        ),
    )
    peaks, masses, picks = (stats[0].reshape(-1), stats[1].reshape(-1), stats[2].reshape(-1))
    peaks, masses, picks = joined((peaks, masses, picks), "dp", combine_parts)
    peak_own = lax.dynamic_slice_in_dim(peaks, dp_rank * own_rows, own_rows)
    mass_own = lax.dynamic_slice_in_dim(masses, dp_rank * own_rows, own_rows)
    pick_own = lax.dynamic_slice_in_dim(picks, dp_rank * own_rows, own_rows)
    token_loss = jnp.log(mass_own) + peak_own - pick_own
    share = lax.all_to_all(encoded, "fsdp", split_axis=1, concat_axis=0, tiled=True)
    every_rows = lax.all_gather(share, "dp", axis=0, tiled=True)
    block_local = assignments - dp_rank * block_width
    partial_share = one_hot_sums(every_rows, block_local, block_width)
    totals = lax.all_to_all(partial_share, "fsdp", split_axis=0, concat_axis=1, tiled=True)
    base = dp_rank * block_width + fsdp_rank * per_dev
    targets = base + jnp.arange(per_dev, dtype=jnp.int32)
    counts = jnp.sum((assignments[:, None] == targets[None, :]).astype(jnp.int32), axis=0)
    previous = lax.dynamic_slice_in_dim(cent_full, fsdp_rank * per_dev, per_dev, 1).T.astype(
        jnp.float32
    )
    new_centroids = jnp.where(
        counts[:, None] > 0, totals / jnp.maximum(counts, 1)[:, None].astype(jnp.float32), previous
    )
    return (token_loss, new_centroids)


def solution(mesh):
    return jax.shard_map(
        shards,
        mesh=mesh,
        in_specs=(
            P("dp"),
            P("fsdp", None),
            P("fsdp", None),
            P("fsdp", None),
            P(),
            P(),
            P("fsdp", "dp"),
            P(),
        ),
        out_specs=(P(("dp", "fsdp")), P(("dp", "fsdp"), None)),
        check_vma=False,
    )
```

profile of v0, /device:TPU:0, one launch (start us, length us, event | category | flops | bytes accessed | tf_op | source)
XLA Modules:
  0.0 482.2 jit_solution(6688410864209391748)
XLA Ops:
  7.2 0.8 fusion.12
  8.1 0.7 compare_and_fusion.1
  8.8 0.2 copy-done
  9.0 5.2 %gather_fusion = bf16[1024,768]{1,0:T(8,128)(2,1)} fusion(bf16[1908,768]{1,0:T(8,128)(2,1)S(1)} %copy-done, s32[1024]{0:T(1024)S(1)} %fusion.12), kind=kCustom, calls=%fused_computation | custom fusion | bytes 3149824 | tf_op jit(solution)/shard_map/jit(_take)/gather | solution.py:89
  14.2 2.8 select_select_fusion
  17.1 0.0 all-gather.10.cloned.1.call-start
  17.1 0.7 all-gather.10.cloned.1.call-update
  17.9 0.7 all-gather.12.cloned.1.call-update
  18.6 0.5 all-gather.14.cloned.1.call-update
  19.2 66.3 %reduce-scatter.2.cloned.1.call-done = bf16[128,768]{1,0:T(8,128)(2,1)} async-done(((bf16[1024,768]{1,0:T(8,128)(2,1)}), bf16[128,768]{1,0:T(8,128)(2,1)}) %reduce-scatter.2.cloned.1.call-update) | async-done | bytes 196624 | tf_op jit(solution)/shard_map/reduce_scatter | solution.py:92
  85.5 65.6 %all-gather.10.cloned.1.call-done = bf16[768,2304]{1,0:T(8,128)(2,1)} async-done(((bf16[96,2304]{1,0:T(8,128)(2,1)}), bf16[768,2304]{1,0:T(8,128)(2,1)}) %all-gather.10.cloned.1.call-update) | async-done | bytes 3538960 | tf_op jit(solution)/shard_map/all_gather | solution.py:97
  151.1 2.8 convolution_convert_fusion
  153.9 1.1 copy.36
  155.0 1.5 fusion.15
  156.5 2.2 convolution_multiply_fusion
  158.7 1.9 convolution_convert_fusion.1
  160.5 32.6 %all-gather.12.cloned.1.call-done = bf16[768,768]{1,0:T(8,128)(2,1)} async-done(((bf16[96,768]{1,0:T(8,128)(2,1)}), bf16[768,768]{1,0:T(8,128)(2,1)}) %all-gather.12.cloned.1.call-update) | async-done | bytes 1179664 | tf_op jit(solution)/shard_map/all_gather | solution.py:98
  193.2 1.7 fusion.16
  194.9 0.2 multiply_reduce_fusion
  195.1 0.1 add_convert_fusion
  195.3 0.8 copy.38
  196.1 3.4 all-to-all-start
  199.5 7.8 %all-to-all-done = bf16[128,8,96]{0,2,1:T(8,128)(2,1)S(1)} async-done(((bf16[128,8,96]{0,2,1:T(8,128)(2,1)}), bf16[128,8,96]{0,2,1:T(8,128)(2,1)S(1)}, u32[]{:S(2)}, u32[]{:S(2)}) %all-to-all-start) | async-done | bytes 196640 | tf_op jit(solution)/shard_map/all_to_all | solution.py:139
  207.3 9.0 %all_gather.31 = bf16[4096,96]{0,1:T(8,128)(2,1)} all-gather(bf16[1024,96]{0,1:T(8,128)(2,1)S(1)} %copy_bitcast_fusion.1), channel_id=1, replica_groups=mesh['dp'=4,'fsdp'=8] {'dp'}, dimensions={0}, use_global_device_ids=true | all-gather | bytes 983040 | tf_op jit(solution)/shard_map/all_gather | solution.py:140
  216.4 2.3 copy.44
  218.6 58.1 %while.37 = (s32[]{:T(128)}, f32[8192,96]{0,1:T(8,128)}, s32[8,512]{1,0:T(8,128)S(1)}, bf16[8,512,96]{2,1,0:T(8,128)(2,1)}, s32[]{:T(128)}, /*index=5*/s32[]{:T(128)}) while((s32[]{:T(128)}, f32[8192,96]{0,1:T(8,128)}, s32[8,512]{1,0:T(8,128)S(1)}, bf16[8,512,96]{2,1,0:T(8,128)(2,1)}, s32[]{:T(128)}, /*index=5*/s32[]{:T(128)}) %tuple.91), condition=%wide.region_12.13_spmd.clone, body=%wide.region_11.12_spmd.clone.sunk | while | flops 811073536 | bytes 6428767 | solution.py:64
  218.6 6.3 %fusion.29 = f32[8192,96]{0,1:T(8,128)} fusion(s32[512]{0:T(512)S(1)} %bitcast.97, f32[8192,96]{0,1:T(8,128)} %get-tuple-element.423, pred[]{:T(512)S(6)} %compare.3, bf16[8,512,96]{2,1,0:T(8,128)(2,1)} %get-tuple-element.431, s32[]{:T(128)S(6)} %copy.73), kind=kOutput, calls=%fused_computation.8.clone.1 | convolution fusion | flops 811073536 | bytes 6424581 | tf_op jit(solution)/shard_map/while/body/eval_jaxpr/dot_general | solution.py:57
  224.9 7.3 %fusion.29 = f32[8192,96]{0,1:T(8,128)} fusion(s32[512]{0:T(512)S(1)} %bitcast.97, f32[8192,96]{0,1:T(8,128)} %get-tuple-element.423, pred[]{:T(512)S(6)} %compare.3, bf16[8,512,96]{2,1,0:T(8,128)(2,1)} %get-tuple-element.431, s32[]{:T(128)S(6)} %copy.73), kind=kOutput, calls=%fused_computation.8.clone.1 | convolution fusion | flops 811073536 | bytes 6424581 | tf_op jit(solution)/shard_map/while/body/eval_jaxpr/dot_general | solution.py:57
  232.3 7.3 %fusion.29 = f32[8192,96]{0,1:T(8,128)} fusion(s32[512]{0:T(512)S(1)} %bitcast.97, f32[8192,96]{0,1:T(8,128)} %get-tuple-element.423, pred[]{:T(512)S(6)} %compare.3, bf16[8,512,96]{2,1,0:T(8,128)(2,1)} %get-tuple-element.431, s32[]{:T(128)S(6)} %copy.73), kind=kOutput, calls=%fused_computation.8.clone.1 | convolution fusion | flops 811073536 | bytes 6424581 | tf_op jit(solution)/shard_map/while/body/eval_jaxpr/dot_general | solution.py:57
  239.6 7.3 %fusion.29 = f32[8192,96]{0,1:T(8,128)} fusion(s32[512]{0:T(512)S(1)} %bitcast.97, f32[8192,96]{0,1:T(8,128)} %get-tuple-element.423, pred[]{:T(512)S(6)} %compare.3, bf16[8,512,96]{2,1,0:T(8,128)(2,1)} %get-tuple-element.431, s32[]{:T(128)S(6)} %copy.73), kind=kOutput, calls=%fused_computation.8.clone.1 | convolution fusion | flops 811073536 | bytes 6424581 | tf_op jit(solution)/shard_map/while/body/eval_jaxpr/dot_general | solution.py:57
  247.0 7.3 %fusion.29 = f32[8192,96]{0,1:T(8,128)} fusion(s32[512]{0:T(512)S(1)} %bitcast.97, f32[8192,96]{0,1:T(8,128)} %get-tuple-element.423, pred[]{:T(512)S(6)} %compare.3, bf16[8,512,96]{2,1,0:T(8,128)(2,1)} %get-tuple-element.431, s32[]{:T(128)S(6)} %copy.73), kind=kOutput, calls=%fused_computation.8.clone.1 | convolution fusion | flops 811073536 | bytes 6424581 | tf_op jit(solution)/shard_map/while/body/eval_jaxpr/dot_general | solution.py:57
  254.3 7.3 %fusion.29 = f32[8192,96]{0,1:T(8,128)} fusion(s32[512]{0:T(512)S(1)} %bitcast.97, f32[8192,96]{0,1:T(8,128)} %get-tuple-element.423, pred[]{:T(512)S(6)} %compare.3, bf16[8,512,96]{2,1,0:T(8,128)(2,1)} %get-tuple-element.431, s32[]{:T(128)S(6)} %copy.73), kind=kOutput, calls=%fused_computation.8.clone.1 | convolution fusion | flops 811073536 | bytes 6424581 | tf_op jit(solution)/shard_map/while/body/eval_jaxpr/dot_general | solution.py:57
  261.6 7.8 %fusion.29 = f32[8192,96]{0,1:T(8,128)} fusion(s32[512]{0:T(512)S(1)} %bitcast.97, f32[8192,96]{0,1:T(8,128)} %get-tuple-element.423, pred[]{:T(512)S(6)} %compare.3, bf16[8,512,96]{2,1,0:T(8,128)(2,1)} %get-tuple-element.431, s32[]{:T(128)S(6)} %copy.73), kind=kOutput, calls=%fused_computation.8.clone.1 | convolution fusion | flops 811073536 | bytes 6424581 | tf_op jit(solution)/shard_map/while/body/eval_jaxpr/dot_general | solution.py:57
  269.4 7.3 %fusion.29 = f32[8192,96]{0,1:T(8,128)} fusion(s32[512]{0:T(512)S(1)} %bitcast.97, f32[8192,96]{0,1:T(8,128)} %get-tuple-element.423, pred[]{:T(512)S(6)} %compare.3, bf16[8,512,96]{2,1,0:T(8,128)(2,1)} %get-tuple-element.431, s32[]{:T(128)S(6)} %copy.73), kind=kOutput, calls=%fused_computation.8.clone.1 | convolution fusion | flops 811073536 | bytes 6424581 | tf_op jit(solution)/shard_map/while/body/eval_jaxpr/dot_general | solution.py:57
  276.8 4.0 copy.55
  280.8 4.5 all-to-all-start.1
  285.3 2.0 convert_reduce_fusion
  287.3 9.2 %all_gather.26 = bf16[512,768]{1,0:T(8,128)(2,1)} all-gather(bf16[128,768]{1,0:T(8,128)(2,1)S(1)} %add_convert_fusion), channel_id=1, replica_groups=mesh['dp'=4,'fsdp'=8] {'dp'}, dimensions={0}, use_global_device_ids=true | all-gather | bytes 983040 | tf_op jit(solution)/shard_map/all_gather | solution.py:106
  296.5 138.5 %all-gather.14.cloned.1.call-done = bf16[768,8192]{1,0:T(8,128)(2,1)} async-done(((bf16[96,8192]{1,0:T(8,128)(2,1)}), bf16[768,8192]{1,0:T(8,128)(2,1)}) %all-gather.14.cloned.1.call-update) | async-done | bytes 12582928 | tf_op jit(solution)/shard_map/all_gather | solution.py:99
  435.0 10.0 %fusion.17 = (f32[512]{0:T(512)S(1)}, f32[512,8192]{1,0:T(8,128)S(1)}) fusion(bf16[512,768]{1,0:T(8,128)(2,1)} %all_gather.26, bf16[768,8192]{1,0:T(8,128)(2,1)} %all-gather.14.cloned.1.call-done), kind=kOutput, calls=%fused_computation.55 | convolution fusion | flops 6446644736 | bytes 30148608 | tf_op jit(solution)/shard_map/while/body/eval_jaxpr/dot_general | solution.py:117
  445.0 5.4 %all-gather.3 = f32[4,1,512]{2,1,0:T(1,128)S(1)} all-gather(f32[1,1,512]{2,1,0:T(1,128)S(1)} %bitcast.102), channel_id=2, replica_groups=mesh['dp'=4,'fsdp'=8] {'dp'}, dimensions={0}, use_global_device_ids=true | all-gather | bytes 10240 | tf_op jit(solution)/shard_map/all_gather | solution.py:14
  450.4 5.6 %select_reduce_fusion = (f32[512]{0:T(512)S(1)}, f32[512]{0:T(512)S(1)}) fusion(f32[512,8192]{1,0:T(8,128)S(1)} %get-tuple-element.309, s32[512]{0:T(512)S(1)} %bitcast.105, f32[512]{0:T(512)S(1)} %get-tuple-element.308), kind=kLoop, calls=%fused_computation.16 | loop fusion | flops 20970496 | bytes 16785408 | tf_op jit(solution)/shard_map/while/body/eval_jaxpr/reduce_sum | solution.py:121
  456.0 5.2 %all-gather.4 = f32[4,1,512]{2,1,0:T(1,128)S(1)} all-gather(f32[1,1,512]{2,1,0:T(1,128)S(1)} %bitcast.104), channel_id=3, replica_groups=mesh['dp'=4,'fsdp'=8] {'dp'}, dimensions={0}, use_global_device_ids=true | all-gather | bytes 10240 | tf_op jit(solution)/shard_map/all_gather | solution.py:14
  461.2 5.2 %all-gather.5 = f32[4,1,512]{2,1,0:T(1,128)S(1)} all-gather(f32[1,1,512]{2,1,0:T(1,128)S(1)} %bitcast.103), channel_id=4, replica_groups=mesh['dp'=4,'fsdp'=8] {'dp'}, dimensions={0}, use_global_device_ids=true | all-gather | bytes 10240 | tf_op jit(solution)/shard_map/all_gather | solution.py:14
  466.4 0.2 while.36
  466.7 4.8 %fusion.9 = f32[1024,768]{0,1:T(8,128)} fusion(f32[8,1024,96]{1,2,0:T(8,128)} %all-to-all-done.1, bf16[768,8192]{1,0:T(8,128)(2,1)} %all-gather.14.cloned.1.call-done, s32[]{:T(128)S(6)} %select_n.52, f32[1024]{0:T(1024)S(1)} %maximum_convert_fusion, pred[1024]{0:T(1024)(128)(4,1)S(1)} %broadcast_compare_fusion), kind=kLoop, calls=%fused_computation.22 | loop fusion | flops 2359296 | bytes 7869444 | tf_op jit(solution)/shard_map/jit(_where)/select_n | solution.py:150
  471.5 3.5 copy.42
  475.0 0.6 dynamic-slice_subtract_fusion.1
  (50 shorter events, 0.4 us)
Async XLA Ops:
  7.2 1.9 copy-start
  7.2 78.3 %reduce-scatter.2.cloned.1.call-start = ((), (), s32[]{:S(2)}) async-start(), calls=%async_computation.3 | async-start | bytes 1769472 | tf_op jit(solution)/shard_map/reduce_scatter | solution.py:92
  17.1 134.0 %all-gather.10.cloned.1.call-start = ((), (), s32[]{:S(2)}) async-start(), calls=%async_computation.4 | async-start | bytes 3981312 | tf_op jit(solution)/shard_map/all_gather | solution.py:97
  17.8 175.3 %all-gather.12.cloned.1.call-start = ((), (), s32[]{:S(2)}) async-start(), calls=%async_computation.5 | async-start | bytes 1327104 | tf_op jit(solution)/shard_map/all_gather | solution.py:98
  18.6 416.4 %all-gather.14.cloned.1.call-start = ((), (), s32[]{:S(2)}) async-start(), calls=%async_computation.6 | async-start | bytes 14155776 | tf_op jit(solution)/shard_map/all_gather | solution.py:99
  154.9 38.2 %copy-start.1 = (bf16[128,768]{1,0:T(8,128)(2,1)S(1)}, bf16[128,768]{1,0:T(8,128)(2,1)}, u32[]{:S(2)}) copy-start(bf16[128,768]{1,0:T(8,128)(2,1)} %reduce-scatter.2.cloned.1.call-done) | copy-start | bytes 589828
  158.7 36.4 %copy-start.3 = (f32[768]{0:T(1024)S(1)}, f32[768]{0:T(1024)}, u32[]{:S(2)}) copy-start(f32[768]{0:T(1024)} %param.17) | copy-start | bytes 9220
  158.7 36.4 %copy-start.4 = (f32[768]{0:T(1024)S(1)}, f32[768]{0:T(1024)}, u32[]{:S(2)}) copy-start(f32[768]{0:T(1024)} %param.16) | copy-start | bytes 9220
  158.7 40.8 %copy-start.2 = (s32[4096]{0:T(1024)S(1)}, s32[4096]{0:T(1024)}, u32[]{:S(2)}) copy-start(s32[4096]{0:T(1024)} %param.19) | copy-start | bytes 49156
  196.1 11.2 %all-to-all-start = ((bf16[128,8,96]{0,2,1:T(8,128)(2,1)}), bf16[128,8,96]{0,2,1:T(8,128)(2,1)S(1)}, u32[]{:S(2)}, u32[]{:S(2)}) async-start(bf16[128,8,96]{0,2,1:T(8,128)(2,1)} %bitcast.18), calls=%async_computation.1 | async-start | bytes 393216 | tf_op jit(solution)/shard_map/all_to_all | solution.py:139
  280.8 185.9 %all-to-all-start.1 = ((f32[8,1024,96]{1,2,0:T(8,128)}), f32[8,1024,96]{1,2,0:T(8,128)}, u32[]{:S(2)}, u32[]{:S(2)}) async-start(f32[8,1024,96]{1,2,0:T(8,128)} %bitcast.84), calls=%async_computation.2 | async-start | bytes 6291456 | tf_op jit(solution)/shard_map/all_to_all | solution.py:143
Sparse Core Ops, SparseCore 0:
  17.2 68.2 reduce-scatter.1
  87.7 63.3 all-gather.9
  153.3 39.8 all-gather.11
  195.2 239.7 all-gather.13
where the time goes:
time: 483 us; the launch traced here: 482 us
  waiting for transfers between devices  313 us (65%)
  matrix products  78.1 us (16%)
  blocking collectives  34 us (7%)
  other arithmetic  17.9 us (4%)
  local copies, waits for them, and re-layouts  17.3 us (4%)
  between operations  14 us (3%)
  starting transfers between devices  8.02 us (2%)
    all_gather x1, waiting for transfers between devices, shards(): lax.all_gather(centroids_t, 'fsdp', axis=0, tiled=True)  139 us
    reduce_scatter x1, waiting for transfers between devices, shards(): lax.psum_scatter(looked, 'fsdp', scatter_dimension=0, tiled=True)  66.3 us
    all_gather x1, waiting for transfers between devices, shards(): lax.all_gather(w_qkv, 'fsdp', axis=0, tiled=True)  65.6 us
    dot_general x8, matrix products, one_visit(): lax.dot_general(hits, block_rows, (((0,), (0,)), ((), ())), preferred_ele...  58.1 us
    all_gather x1, waiting for transfers between devices, shards(): lax.all_gather(w_out, 'fsdp', axis=0, tiled=True)  32.6 us
    all_gather x3, blocking collectives, joined(): everything = jax.tree.map(lambda part: lax.all_gather(part, axis), shard)  15.7 us
    dot_general x1, matrix products, body_visit(): logits = jnp.dot(block_rows, cent_full, preferred_element_type=jnp.float32)  9.99 us
  transfers between devices with their start and end apart: 6, of which 5 were waited for; matrix products, arithmetic and copies ran while one was open for 20% of the time, Pallas kernels for 0%

commit v1 on v0

--- a/solution.py
+++ b/solution.py
@@ -1,8 +1,11 @@
+import functools
 import math
 
 import jax
 import jax.numpy as jnp
 from jax import lax
+from jax.experimental import pallas as pl
+from jax.experimental.pallas import tpu as pltpu
 from jax.sharding import PartitionSpec as P
 
 HEADS = 12
@@ -153,9 +156,371 @@
     return (token_loss, new_centroids)
 
 
+VMEM_LIMIT = 60 * 1024 * 1024
+WHOLE_VMEM = pl.BlockSpec(memory_space=pltpu.VMEM)
+
+
+class Place:
+    def __init__(self, deep):
+        self.deep = deep
+        self.dp, self.fsdp = lax.axis_index("dp"), lax.axis_index("fsdp")
+        self.x, self.c = self.dp // 2, self.dp % 2
+        self.z, self.y = self.fsdp // 2, self.fsdp % 2
+
+    def at(self, x=None, c=None, z=None, y=None):
+        x, c = self.x if x is None else x, self.c if c is None else c
+        z, y = self.z if z is None else z, self.y if y is None else y
+        return {"dp": x * 2 + c, "fsdp": z * 2 + y}
+
+    def greet(self):
+        barrier = pltpu.get_barrier_semaphore()
+        peers = [self.at(x=1 - self.x), self.at(c=1 - self.c), self.at(y=1 - self.y)]
+        peers += [self.at(z=(self.z + k) % self.deep) for k in range(1, self.deep)]
+        for peer in peers:
+            pl.semaphore_signal(barrier, inc=1, device_id=peer, device_id_type=pl.DeviceIdType.MESH)
+        pl.semaphore_wait(barrier, len(peers))
+
+
+class Sender:
+    def __init__(self, sems):
+        self.sems, self.used, self.sent = sems, 0, []
+
+    def send(self, src, dst, recv_sem, peer, when=None):
+        copy = pltpu.make_async_remote_copy(
+            src_ref=src,
+            dst_ref=dst,
+            send_sem=self.sems.at[self.used],
+            recv_sem=recv_sem,
+            device_id=peer,
+            device_id_type=pl.DeviceIdType.MESH,
+        )
+        self.used += 1
+        self.sent.append((copy, when))
+        guarded(when, copy.start)
+
+    def arrived(self, dst, recv_sem, peer, when=None):
+        copy = pltpu.make_async_remote_copy(
+            src_ref=dst,
+            dst_ref=dst,
+            send_sem=self.sems.at[0],
+            recv_sem=recv_sem,
+            device_id=peer,
+            device_id_type=pl.DeviceIdType.MESH,
+        )
+        guarded(when, copy.wait_recv)
+
+    def drain(self):
+        for copy, when in self.sent:
+            guarded(when, copy.wait_send)
+
+
+def guarded(when, action):
+    if when is None:
+        action()
+    else:
+        pl.when(when)(action)
+
+
+def prepare_kernel(
+    deep, rows_ref, mine_ref, inputs_ref, w_ref, from_y, joined_y, from_z, send_sems, y_sems, z_sems, w_sems
+):
+    place = Place(deep)
+    place.greet()
+    out = Sender(send_sems)
+    x, c, z, y = place.x, place.c, place.z, place.y
+    quarter, across = x * 2 + c, (1 - x) * 2 + c
+    own = place.fsdp
+    for k in range(1, deep + 1):
+        to = (z + k) % deep
+        out.send(rows_ref.at[to * 2 + (1 - y)], from_y.at[to], y_sems.at[to], place.at(y=1 - y))
+    up, down = place.at(z=jnp.minimum(z + 1, deep - 1)), place.at(z=jnp.maximum(z - 1, 0))
+
+    def share(q, s, src, to_y):
+        if to_y:
+            out.send(src, w_ref.at[q, s], w_sems.at[q, s], place.at(y=1 - y))
+
+    mine = mine_ref.at[quarter]
+    out.send(mine, w_ref.at[quarter, own], w_sems.at[quarter, own], up, z + 1 < deep)
+    out.send(mine, w_ref.at[quarter, own], w_sems.at[quarter, own], down, z > 0)
+
+    def spread(s, when=None):
+        block = w_ref.at[quarter, s]
+        out.send(block, block, w_sems.at[quarter, s], place.at(x=1 - x), when)
+        out.send(block, block, w_sems.at[quarter, s], place.at(c=1 - c), when)
+
+    for k in range(1, deep):
+        for sign in (-1, 1):
+            have = (z + sign * k >= 0) & (z + sign * k < deep)
+            z0 = jnp.clip(z + sign * k, 0, deep - 1)
+            s = z0 * 2 + y
+            block = w_ref.at[quarter, s]
+            out.arrived(block, w_sems.at[quarter, s], place.at(y=1 - y), have)
+            onward = have & (z + 1 < deep) if sign < 0 else have & (z > 0)
+            if k < deep - 1:
+                out.send(block, block, w_sems.at[quarter, s], up if sign < 0 else down, onward)
+            spread(s, have)
+    for q in range(4):
+        w_ref[q, own] = mine_ref[q]
+    for k in range(1, deep + 1):
+        to = (z + k) % deep
+        out.arrived(from_y.at[to], y_sems.at[to], place.at(y=1 - y))
+        if k < deep:
+            joined_y[to] = from_y[to] + rows_ref[to * 2 + y]
+            out.send(joined_y.at[to], from_z.at[deep - k], z_sems.at[deep - k], place.at(z=to))
+    out.send(mine, w_ref.at[quarter, own], w_sems.at[quarter, own], place.at(y=1 - y))
+    for k in range(1, deep):
+        s = (z + k) % deep * 2 + y
+        block = w_ref.at[quarter, s]
+        out.send(block, block, w_sems.at[quarter, s], place.at(y=1 - y))
+    for k in range(deep):
+        s = (z + k) % deep * 2 + (1 - y)
+        out.arrived(w_ref.at[quarter, s], w_sems.at[quarter, s], place.at(y=1 - y))
+        spread(s)
+    others = [(z + k) % deep * 2 + y for k in range(1, deep)]
+    others += [(z + k) % deep * 2 + (1 - y) for k in range(deep)]
+    for s in others:
+        block = w_ref.at[across, s]
+        out.arrived(block, w_sems.at[across, s], place.at(x=1 - x))
+        out.send(block, block, w_sems.at[across, s], place.at(c=1 - c))
+    total = from_y[z] + rows_ref[own]
+    for k in range(1, deep):
+        out.arrived(from_z.at[k], z_sems.at[k], place.at(y=1 - y))
+        total = total + from_z[k]
+    inputs_ref[...] = total
+    for q in (x * 2 + (1 - c), (1 - x) * 2 + (1 - c)):
+        for s in others:
+            out.arrived(w_ref.at[q, s], w_sems.at[q, s], place.at(c=1 - c))
+    out.drain()
+
+
+def prepare(rows, mine, deep):
+    parts, own_rows, width = rows.shape
+    feats = mine.shape[1]
+    return pl.pallas_call(
+        functools.partial(prepare_kernel, deep),
+        out_shape=(
+            jax.ShapeDtypeStruct((own_rows, width), rows.dtype),
+            jax.ShapeDtypeStruct((4, parts, feats, width), mine.dtype),
+        ),
+        in_specs=[WHOLE_VMEM] * 2,
+        out_specs=(WHOLE_VMEM, WHOLE_VMEM),
+        scratch_shapes=[
+            pltpu.VMEM((deep, own_rows, width), rows.dtype),
+            pltpu.VMEM((deep, own_rows, width), rows.dtype),
+            pltpu.VMEM((deep, own_rows, width), rows.dtype),
+            pltpu.SemaphoreType.DMA((16 * deep,)),
+            pltpu.SemaphoreType.DMA((deep,)),
+            pltpu.SemaphoreType.DMA((deep,)),
+            pltpu.SemaphoreType.DMA((4, parts)),
+        ],
+        compiler_params=pltpu.CompilerParams(
+            collective_id=0, has_side_effects=True, vmem_limit_bytes=VMEM_LIMIT
+        ),
+        name="prepare",
+    )(rows, mine)
+
+
+def tokens_kernel(deep, mine_ref, all_ref, send_sems, recv_sems):
+    place = Place(deep)
+    place.greet()
+    out = Sender(send_sems)
+    x, c, z, y = place.x, place.c, place.z, place.y
+    x_first = c == 1
+    second_xy = (jnp.where(x_first, 1 - x, x), jnp.where(x_first, y, 1 - y))
+    third_xy = (jnp.where(x_first, x, 1 - x), jnp.where(x_first, 1 - y, y))
+    second = place.at(x=second_xy[0], y=second_xy[1])
+    third = place.at(x=third_xy[0], y=third_xy[1])
+    partner = place.at(c=1 - c)
+    up, down = place.at(z=jnp.minimum(z + 1, deep - 1)), place.at(z=jnp.maximum(z - 1, 0))
+
+    def number(x0, c0, z0, y0):
+        return ((x0 * 2 + c0) * deep + z0) * 2 + y0
+
+    def push(b, peer, when=None, src=None):
+        block = all_ref.at[b]
+        out.send(block if src is None else src, block, recv_sems.at[b], peer, when)
+
+    def wait(b, when=None):
+        out.arrived(all_ref.at[b], recv_sems.at[b], partner, when)
+
+    own = number(x, c, z, y)
+    push(own, up, z + 1 < deep, mine_ref)
+    push(own, down, z > 0, mine_ref)
+    for peer in (second, third, partner):
+        push(own, peer, None, mine_ref)
+    all_ref[own] = mine_ref[...]
+    order = [(z, None, 0)]
+    for k in range(1, deep):
+        for sign in (-1, 1):
+            have = (z + sign * k >= 0) & (z + sign * k < deep)
+            order.append((jnp.clip(z + sign * k, 0, deep - 1), have, sign))
+    for at, (z0, have, sign) in enumerate(order):
+        if at > 0:
+            b = number(x, c, z0, y)
+            wait(b, have)
+            if at + 2 < len(order):
+                push(b, up if sign < 0 else down, have & ((z + 1 < deep) if sign < 0 else (z > 0)))
+            push(b, second, have)
+            push(b, third, have)
+            push(b, partner, have)
+        b = number(second_xy[0], c, z0, second_xy[1])
+        wait(b, have)
+        push(b, third, have)
+        push(b, partner, have)
+        lag = [order[at - 2]] if at >= 2 else []
+        lag += order[-2:] if at == len(order) - 1 else []
+        for z1, have1, unused in lag:
+            for second_way in (False, True):
+                xx, yy = third_xy
+                if second_way:
+                    xx, yy = 1 - x, 1 - y
+                b = number(xx, c, z1, yy)
+                wait(b, have1)
+                push(b, partner, have1)
+    for k in range(deep):
+        for x0 in range(2):
+            for y0 in range(2):
+                wait(number(x0, 1 - c, k, y0))
+    out.drain()
+
+
+def every_token(mine, deep):
+    rows, width = mine.shape
+    blocks = 8 * deep
+    return pl.pallas_call(
+        functools.partial(tokens_kernel, deep),
+        out_shape=jax.ShapeDtypeStruct((blocks, rows, width), mine.dtype),
+        in_specs=[WHOLE_VMEM],
+        out_specs=WHOLE_VMEM,
+        scratch_shapes=[
+            pltpu.SemaphoreType.DMA((24 * deep,)),
+            pltpu.SemaphoreType.DMA((blocks,)),
+        ],
+        compiler_params=pltpu.CompilerParams(
+            collective_id=1, has_side_effects=True, vmem_limit_bytes=VMEM_LIMIT
+        ),
+        name="every_token",
+    )(mine)
+
+
+def owner_kernel(steps, assign_ref, tokens_ref, cent_ref, peak_ref, mass_ref, pick_ref, new_ref, old, counts):
+    step = pl.program_id(0)
+
+    @pl.when(step == 0)
+    def first():
+        old[...] = cent_ref[...].T
+        new_ref[...] = jnp.zeros_like(new_ref)
+        counts[...] = jnp.zeros_like(counts)
+
+    rows = tokens_ref[...]
+    logits = lax.dot_general(
+        old[...], rows, (((1,), (1,)), ((), ())), preferred_element_type=jnp.float32
+    )
+    peak = jnp.max(logits, axis=0, keepdims=True)
+    peak_ref[0] = peak
+    mass_ref[0] = jnp.sum(jnp.exp(logits - peak), axis=0, keepdims=True)
+    hits = lax.broadcasted_iota(jnp.int32, logits.shape, 0) == assign_ref[0]
+    pick_ref[0] = jnp.sum(jnp.where(hits, logits, 0.0), axis=0, keepdims=True)
+    ones = jnp.where(hits, 1.0, 0.0)
+    counts[...] += jnp.sum(ones, axis=1, keepdims=True)
+    new_ref[...] += jnp.dot(ones.astype(jnp.bfloat16), rows, preferred_element_type=jnp.float32)
+
+    @pl.when(step == steps - 1)
+    def last():
+        many = counts[...]
+        new_ref[...] = jnp.where(
+            many > 0, new_ref[...] / jnp.maximum(many, 1.0), old[...].astype(jnp.float32)
+        )
+
+
+def owner(tokens, cent, local_assign):
+    count, width = tokens.shape
+    per_dev = cent.shape[1]
+    block = math.gcd(count, 512)
+    steps = count // block
+    row = pl.BlockSpec((1, 1, block), lambda i: (i, 0, 0))
+    stat = jax.ShapeDtypeStruct((steps, 1, block), jnp.float32)
+    peak, mass, pick, new = pl.pallas_call(
+        functools.partial(owner_kernel, steps),
+        out_shape=(stat, stat, stat, jax.ShapeDtypeStruct((per_dev, width), jnp.float32)),
+        grid=(steps,),
+        in_specs=[
+            row,
+            pl.BlockSpec((block, width), lambda i: (i, 0)),
+            pl.BlockSpec((width, per_dev), lambda i: (0, 0)),
+        ],
+        out_specs=(row, row, row, pl.BlockSpec((per_dev, width), lambda i: (0, 0))),
+        scratch_shapes=[
+            pltpu.VMEM((per_dev, width), cent.dtype),
+            pltpu.VMEM((per_dev, 1), jnp.float32),
+        ],
+        compiler_params=pltpu.CompilerParams(vmem_limit_bytes=VMEM_LIMIT),
+        name="owner",
+    )(local_assign.reshape(steps, 1, block), tokens, cent)
+    return peak.reshape(-1), mass.reshape(-1), pick.reshape(-1), new
+
+
+def token_shards(token_ids, embed_table, w_qkv, w_out, ln_gain, ln_bias, centroids_t, assignments):
+    dp_size, fsdp_size = lax.axis_size("dp"), lax.axis_size("fsdp")
+    dp_rank, fsdp_rank = lax.axis_index("dp"), lax.axis_index("fsdp")
+    deep = fsdp_size // 2
+    vocab_rows, width = embed_table.shape
+    own_rows = token_ids.shape[0] // fsdp_size
+    local_ids = token_ids - fsdp_rank * vocab_rows
+    inside = (local_ids >= 0) & (local_ids < vocab_rows)
+    looked = jnp.take(embed_table, jnp.clip(local_ids, 0, vocab_rows - 1), axis=0)
+    looked = jnp.where(inside[:, None], looked, jnp.zeros_like(looked))
+    rows = looked.reshape(fsdp_size, own_rows, width)
+    mine = jnp.stack([*jnp.split(w_qkv, 3, axis=1), w_out])
+    inputs, weights = prepare(rows, mine, deep)
+    inputs, weights, centroids_t = lax.optimization_barrier((inputs, weights, centroids_t))
+    cent = lax.all_to_all(centroids_t, "fsdp", split_axis=1, concat_axis=0, tiled=True)
+    weights = weights.reshape(4, width, width)
+    encoded = encode_quarters(inputs, weights, ln_gain, ln_bias)
+    tokens = every_token(encoded, deep).reshape(-1, width)
+    per_dev = cent.shape[1]
+    base = (dp_rank * fsdp_size + fsdp_rank) * per_dev
+    peak, mass, pick, new = owner(tokens, cent, assignments - base)
+    stats = jnp.stack([peak, mass, pick]).reshape(3, dp_size * fsdp_size, own_rows).transpose(1, 0, 2)
+    stats = lax.all_to_all(stats, ("dp", "fsdp"), split_axis=0, concat_axis=0, tiled=True)
+    top = jnp.max(stats[:, 0], axis=0)
+    total = jnp.sum(stats[:, 1] * jnp.exp(stats[:, 0] - top[None]), axis=0)
+    return jnp.log(total) + top - jnp.sum(stats[:, 2], axis=0), new
+
+
+def encode_quarters(inputs, weights, ln_gain, ln_bias):
+    passages = inputs.shape[0] // SEQ
+
+    def heads(q):
+        part = jnp.dot(inputs, weights[q], preferred_element_type=jnp.float32).astype(jnp.bfloat16)
+        return part.reshape(passages, SEQ, HEADS, HEAD)
+
+    scores = jnp.einsum(
+        "bqhd,bkhd->bhqk", heads(0), heads(1), preferred_element_type=jnp.float32
+    ) * (1.0 / math.sqrt(HEAD))
+    probs = jax.nn.softmax(scores, axis=-1).astype(jnp.bfloat16)
+    context = jnp.einsum("bhqk,bkhd->bqhd", probs, heads(2), preferred_element_type=jnp.float32)
+    context = context.astype(jnp.bfloat16).reshape(inputs.shape[0], HEADS * HEAD)
+    mixed = jnp.dot(context, weights[3], preferred_element_type=jnp.float32) + inputs.astype(
+        jnp.float32
+    )
+    return layer_norm(mixed, ln_gain, ln_bias).astype(jnp.bfloat16)
+
+
+def plan(mesh):
+    dp_size, fsdp_size = mesh.shape["dp"], mesh.shape["fsdp"]
+
+    def either(*args):
+        few_tokens = args[7].shape[0] <= args[6].shape[1]
+        paired = dp_size == 4 and fsdp_size % 2 == 0
+        return token_shards(*args) if few_tokens and paired else shards(*args)
+
+    return either
+
+
 def solution(mesh):
     return jax.shard_map(
-        shards,
+        plan(mesh),
         mesh=mesh,
         in_specs=(
             P("dp"),

time: 483 us -> 177 us (0.37)
  waiting for transfers between devices: 313 us -> 0.01 us
  Pallas kernels: 0 us -> 124 us
  matrix products: 78.1 us -> 11.3 us
  blocking collectives: 34 us -> 11.1 us
  between operations: 14 us -> 0.79 us
  other arithmetic: 17.9 us -> 8.01 us
    all_gather x3 -> x0, waiting for transfers between devices: 237 us -> none  [the longest x1 139 us: shards(): lax.all_gather(centroids_t, 'fsdp', axis=0, tiled=True)]
    pallas_call x0 -> x3, Pallas kernels: none -> 124 us  [the longest x1 54.3 us: every_token(): pl.pallas_call(functools.partial(tokens_kernel, deep), out_shape=jax.Shap...]
    reduce_scatter x1 -> x0, waiting for transfers between devices: 66.3 us -> none  [shards(): lax.psum_scatter(looked, 'fsdp', scatter_dimension=0, tiled=True)]
    dot_general x13 -> x6, matrix products: 76.6 us -> 10.9 us  [the longest x3 6.16 us: heads(): jnp.dot(inputs, weights[q], preferred_element_type=jnp.float32)]
    all_gather x5 -> x0, blocking collectives: 34 us -> none  [the longest x3 15.7 us: joined(): everything = jax.tree.map(lambda part: lax.all_gather(part, axis), shard)]
    all_to_all x0 -> x1, blocking collectives: none -> 11.1 us  [token_shards(): lax.all_to_all(stats, ('dp', 'fsdp'), split_axis=0, concat_axis=0, tiled=...]
    all_to_all x2 -> x1, waiting for transfers between devices: 7.77 us -> 0.01 us  [token_shards(): lax.all_to_all(centroids_t, 'fsdp', split_axis=1, concat_axis=0, tiled=True)]
    reduce_sum x2 -> x1, other arithmetic: 7.59 us -> 0.03 us  [token_shards(): total = jnp.sum(stats[:, 1] * jnp.exp(stats[:, 0] - top[None]), axis=0)]
  transfers between devices with their start and end apart: 6 -> 1, of which waited for: 5 -> 0; matrix products, arithmetic and copies ran while one was open for 20% -> 12% of each run, Pallas kernels for 0% -> 31%
where the time goes in v1:
time: 177 us
  Pallas kernels  124 us (70%)
  local copies, waits for them, and re-layouts  16.7 us (9%)
  matrix products  11.3 us (6%)
  blocking collectives  11.1 us (6%)
  other arithmetic  8.01 us (5%)
  starting transfers between devices  4.29 us (2%)
    pallas_call x1, Pallas kernels, every_token(): pl.pallas_call(functools.partial(tokens_kernel, deep), out_shape=jax.Shap...  54.3 us
    pallas_call x1, Pallas kernels, prepare(): pl.pallas_call(functools.partial(prepare_kernel, deep), out_shape=(jax.Sh...  48.2 us
    pallas_call x1, Pallas kernels, owner(): pl.pallas_call(functools.partial(owner_kernel, steps), out_shape=(stat, s...  21.8 us
    all_to_all x1, blocking collectives, token_shards(): lax.all_to_all(stats, ('dp', 'fsdp'), split_axis=0, concat_axis=0, tiled=...  11.1 us
    dot_general x3, matrix products, heads(): jnp.dot(inputs, weights[q], preferred_element_type=jnp.float32)  6.16 us
    gather x1, local copies, waits for them, and re-layouts, token_shards(): jnp.take(embed_table, jnp.clip(local_ids, 0, vocab_rows - 1), axis=0)  5.21 us
    slice x1, local copies, waits for them, and re-layouts, encode_quarters(): weights[3]  4.72 us
    all_to_all x1, starting transfers between devices, token_shards(): lax.all_to_all(centroids_t, 'fsdp', split_axis=1, concat_axis=0, tiled=True)  4.29 us
  transfers between devices with their start and end apart: 1, of which 0 were waited for; matrix products, arithmetic and copies ran while one was open for 12% of the time, Pallas kernels for 31%

profile of v1, /device:TPU:0, one launch (start us, length us, event | category | flops | bytes accessed | tf_op | source)
XLA Modules:
  0.0 176.5 jit_solution(3153478340297276473)
XLA Ops:
  0.6 0.0 copy-start
  0.7 0.8 and_bitcast_fusion.1
  1.5 0.7 fusion.3
  2.2 1.1 slice_bitcast_fusion.2
  3.3 0.0 copy-done
  3.3 5.2 %gather_fusion = bf16[1024,768]{1,0:T(8,128)(2,1)} fusion(bf16[1908,768]{1,0:T(8,128)(2,1)S(1)} %copy-done, s32[1024]{0:T(1024)S(1)} %fusion.3), kind=kCustom, calls=%fused_computation | custom fusion | bytes 3149824 | tf_op jit(solution)/shard_map/jit(_take)/gather | solution.py:471
  8.5 0.0 copy-start.2
  8.5 2.5 %select_select_fusion.rows_ref = bf16[8,128,768]{2,1,0:T(8,128)(2,1)} fusion(bf16[8,128,768]{2,1,0:T(8,128)(2,1)} %bitcast.64, pred[8,128]{1,0:T(8,128)(4,1)S(1)} %get-tuple-element.32, pred[8,128]{1,0:T(8,128)(4,1)S(1)} %get-tuple-element.31), kind=kLoop, calls=%fused_computation.3 | loop fusion | flops 1572864 | bytes 3147776 | tf_op jit(solution)/shard_map/jit(_where)/select_n | solution.py:472
  11.1 0.0 copy-done.2
  11.1 0.9 pad_maximum_fusion.mine_ref
  11.9 48.2 %prepare.1 = (bf16[128,768]{1,0:T(8,128)(2,1)}, bf16[4,8,96,768]{3,2,1,0:T(8,128)(2,1)}) custom-call(bf16[8,128,768]{2,1,0:T(8,128)(2,1)} %select_select_fusion.rows_ref, bf16[4,96,768]{2,1,0:T(8,128)(2,1)} %pad_maximum_fusion.mine_ref), custom_call_target="tpu_custom_call" | custom-call | tf_op jit(solution)/shard_map/prepare/pallas_call | solution.py:299
  60.1 2.7 %copy.33 = bf16[12,8,8,1024]{3,2,0,1:T(8,128)(2,1)} copy(bf16[12,8,8,1024]{3,2,1,0:T(8,128)(2,1)} %bitcast.69) | data formatting | bytes 3145728 | tf_op jit(solution)/shard_map/all_to_all | solution.py:477
  62.8 4.3 %all-to-all-start = ((bf16[96,8,1024]{2,0,1:T(8,128)(2,1)}), bf16[96,8,1024]{2,0,1:T(8,128)(2,1)}, u32[]{:S(2)}, u32[]{:S(2)}) async-start(bf16[96,8,1024]{2,0,1:T(8,128)(2,1)} %bitcast.63), calls=%async_computation | async-start | bytes 3145728 | tf_op jit(solution)/shard_map/all_to_all | solution.py:477
  67.1 0.0 copy-start.1
  67.1 4.7 %fusion.6 = (bf16[1,8,96,768]{3,2,1,0:T(8,128)(2,1)}, bf16[1,8,96,768]{3,2,1,0:T(8,128)(2,1)}, bf16[1,8,96,768]{3,2,1,0:T(8,128)(2,1)}, bf16[1,8,96,768]{3,2,1,0:T(8,128)(2,1)}) fusion(bf16[4,8,96,768]{3,2,1,0:T(8,128)(2,1)} %get-tuple-element.14), kind=kLoop, calls=%fused_computation.33 | loop fusion | bytes 9437184 | tf_op jit(solution)/shard_map/slice | solution.py:504
  71.9 0.0 copy-done.1
  71.9 1.6 convolution_convert_fusion.1
  73.5 0.2 copy.22
  73.6 2.3 %convolution_convert_fusion.2 = bf16[128,768]{1,0:T(8,128)(2,1)} fusion(bf16[128,768]{1,0:T(8,128)(2,1)S(1)} %copy-done.1, bf16[768,768]{1,0:T(8,128)(2,1)} %bitcast.67), kind=kOutput, calls=%fused_computation.10 | convolution fusion | flops 151093248 | bytes 1572864 | tf_op jit(solution)/shard_map/dot_general | solution.py:495
  75.9 1.1 copy.21
  77.0 2.3 %convolution_convert_fusion.3 = bf16[128,768]{1,0:T(8,128)(2,1)} fusion(bf16[128,768]{1,0:T(8,128)(2,1)S(1)} %copy-done.1, bf16[768,768]{1,0:T(8,128)(2,1)} %bitcast.66), kind=kOutput, calls=%fused_computation.11 | convolution fusion | flops 151093248 | bytes 1572864 | tf_op jit(solution)/shard_map/dot_general | solution.py:495
  79.3 1.7 copy.20
  81.0 0.4 fusion.7
  81.5 1.2 convolution_multiply_fusion
  82.7 1.8 %convolution_convert_fusion = bf16[12,64,128]{2,1,0:T(8,128)(2,1)S(1)} fusion(bf16[128,12,64]{0,2,1:T(8,128)(2,1)} %bitcast.75, f32[12,128]{1,0:T(8,128)S(1)} %fusion.7, f32[12,128,128]{1,2,0:T(8,128)} %convolution_multiply_fusion), kind=kOutput, calls=%fused_computation.8 | convolution fusion | flops 25855616 | bytes 1185792 | tf_op jit(solution)/shard_map/bhqk,bkhd->bqhd/dot_general | solution.py:502
  84.4 0.0 copy-start.4
  84.5 0.0 copy-start.5
  84.5 1.7 fusion.8
  86.2 0.2 multiply_reduce_fusion
  86.4 0.0 copy-done.4
  86.4 0.0 copy-done.5
  86.4 0.8 add_convert_fusion.mine_ref
  87.2 0.0 copy-start.3
  87.3 54.3 %every_token.1 = bf16[32,128,768]{2,1,0:T(8,128)(2,1)} custom-call(bf16[128,768]{1,0:T(8,128)(2,1)} %add_convert_fusion.mine_ref), custom_call_target="tpu_custom_call" | custom-call | tf_op jit(solution)/shard_map/every_token/pallas_call | solution.py:390
  141.6 0.0 copy-done.3
  141.6 0.6 broadcast_subtract_fusion
  142.2 0.0 all-to-all-done
  142.2 21.8 %owner.1 = (f32[8,1,512]{2,1,0:T(1,128)}, f32[8,1,512]{2,1,0:T(1,128)}, f32[8,1,512]{2,1,0:T(1,128)}, f32[1024,768]{1,0:T(8,128)}) custom-call(s32[8,1,512]{2,1,0:T(1,128)} %bitcast.77, bf16[4096,768]{1,0:T(8,128)(2,1)} %bitcast.62, bf16[768,1024]{1,0:T(8,128)(2,1)} %bitcast.20.cent_ref), custom_call_target="tpu_custom_call" | custom-call | tf_op jit(solution)/shard_map/owner/pallas_call | solution.py:443
  164.0 0.8 maximum_bitcast_fusion
  164.8 11.1 %all_to_all.24 = f32[32,3,128]{2,1,0:T(4,128)S(1)} all-to-all(f32[32,3,128]{2,1,0:T(4,128)S(1)} %maximum_bitcast_fusion), channel_id=1, replica_groups=mesh['dp'=4,'fsdp'=8] {'dp','fsdp'}, dimensions={0} | all-to-all | bytes 98304 | tf_op jit(solution)/shard_map/all_to_all | solution.py:485
  175.9 0.1 slice_reduce_fusion.1
  176.0 0.5 add_subtract_fusion
  (3 shorter events, 0.0 us)
Async XLA Ops:
  0.6 2.7 %copy-start = (bf16[1908,768]{1,0:T(8,128)(2,1)S(1)}, bf16[1908,768]{1,0:T(8,128)(2,1)}, u32[]{:S(2)}) copy-start(bf16[1908,768]{1,0:T(8,128)(2,1)} %param.9) | copy-start | bytes 8792068
  8.5 2.5 %copy-start.2 = (bf16[96,768]{1,0:T(8,128)(2,1)S(1)}, bf16[96,768]{1,0:T(8,128)(2,1)}, u32[]{:S(2)}) copy-start(bf16[96,768]{1,0:T(8,128)(2,1)} %param.11) | copy-start | bytes 442372
  62.8 79.3 %all-to-all-start = ((bf16[96,8,1024]{2,0,1:T(8,128)(2,1)}), bf16[96,8,1024]{2,0,1:T(8,128)(2,1)}, u32[]{:S(2)}, u32[]{:S(2)}) async-start(bf16[96,8,1024]{2,0,1:T(8,128)(2,1)} %bitcast.63), calls=%async_computation | async-start | bytes 3145728 | tf_op jit(solution)/shard_map/all_to_all | solution.py:477
  67.1 4.7 %copy-start.1 = (bf16[128,768]{1,0:T(8,128)(2,1)S(1)}, bf16[128,768]{1,0:T(8,128)(2,1)}, u32[]{:S(2)}) copy-start(bf16[128,768]{1,0:T(8,128)(2,1)} %get-tuple-element.13) | copy-start | bytes 589828
  84.4 2.0 %copy-start.4 = (f32[768]{0:T(1024)S(1)}, f32[768]{0:T(1024)}, u32[]{:S(2)}) copy-start(f32[768]{0:T(1024)} %param.13) | copy-start | bytes 9220
  84.5 2.0 %copy-start.5 = (f32[768]{0:T(1024)S(1)}, f32[768]{0:T(1024)}, u32[]{:S(2)}) copy-start(f32[768]{0:T(1024)} %param.12) | copy-start | bytes 9220
  87.2 54.3 %copy-start.3 = (s32[4096]{0:T(1024)S(1)}, s32[4096]{0:T(1024)}, u32[]{:S(2)}) copy-start(s32[4096]{0:T(1024)} %param.15) | copy-start | bytes 49156

commit v2 on v0

--- a/solution.py
+++ b/solution.py
@@ -1,8 +1,11 @@
+import functools
 import math
 
 import jax
 import jax.numpy as jnp
 from jax import lax
+from jax.experimental import pallas as pl
+from jax.experimental.pallas import tpu as pltpu
 from jax.sharding import PartitionSpec as P
 
 HEADS = 12
@@ -153,9 +156,459 @@
     return (token_loss, new_centroids)
 
 
+VMEM_LIMIT = 60 * 1024 * 1024
+WHOLE_VMEM = pl.BlockSpec(memory_space=pltpu.VMEM)
+
+
+class Place:
+    def __init__(self, deep):
+        self.deep = deep
+        self.dp, self.fsdp = lax.axis_index("dp"), lax.axis_index("fsdp")
+        self.x, self.c = self.dp // 2, self.dp % 2
+        self.z, self.y = self.fsdp // 2, self.fsdp % 2
+
+    def at(self, x=None, c=None, z=None, y=None):
+        x, c = self.x if x is None else x, self.c if c is None else c
+        z, y = self.z if z is None else z, self.y if y is None else y
+        return {"dp": x * 2 + c, "fsdp": z * 2 + y}
+
+    def greet(self):
+        barrier = pltpu.get_barrier_semaphore()
+        everyone = 8 * self.deep
+        me = self.dp * 2 * self.deep + self.fsdp
+
+        @pl.loop(1, everyone)
+        def each(k):
+            peer = (me + k) % everyone
+            there = {"dp": peer // (2 * self.deep), "fsdp": peer % (2 * self.deep)}
+            pl.semaphore_signal(barrier, inc=1, device_id=there, device_id_type=pl.DeviceIdType.MESH)
+
+        pl.semaphore_wait(barrier, everyone - 1)
+
+
+class Sender:
+    def __init__(self, sems):
+        self.sems, self.used, self.sent = sems, 0, []
+
+    def send(self, src, dst, recv_sem, peer, when=None):
+        copy = pltpu.make_async_remote_copy(
+            src_ref=src,
+            dst_ref=dst,
+            send_sem=self.sems.at[self.used],
+            recv_sem=recv_sem,
+            device_id=peer,
+            device_id_type=pl.DeviceIdType.MESH,
+        )
+        self.used += 1
+        self.sent.append((copy, when))
+        guarded(when, copy.start)
+
+    def arrived(self, dst, recv_sem, peer, when=None):
+        copy = pltpu.make_async_remote_copy(
+            src_ref=dst,
+            dst_ref=dst,
+            send_sem=self.sems.at[0],
+            recv_sem=recv_sem,
+            device_id=peer,
+            device_id_type=pl.DeviceIdType.MESH,
+        )
+        guarded(when, copy.wait_recv)
+
+    def drain(self):
+        for copy, when in self.sent:
+            guarded(when, copy.wait_send)
+
+
+def guarded(when, action):
+    if when is None:
+        action()
+    else:
+        pl.when(when)(action)
+
+
+def near_first(z, k, deep):
+    below, above = z, deep - 1 - z
+    both = jnp.minimum(below, above)
+    swing = z - (k + 1) // 2 if k % 2 else z + k // 2
+    far = jnp.where(above > below, z + k - both, z - k + both)
+    return jnp.where(k <= 2 * both, swing, far)
+
+
+def passage(x, quarters, gain, bias, w_ref):
+    width = x.shape[1]
+
+    def dense(rows, q):
+        weights = w_ref[q].reshape(width, width)
+        return jnp.dot(rows, weights, preferred_element_type=jnp.float32)
+
+    query, key, value = (dense(x, q).astype(jnp.bfloat16) for q in quarters[:3])
+    context = []
+    for head in range(HEADS):
+        at = slice(head * HEAD, (head + 1) * HEAD)
+        scores = lax.dot_general(
+            query[:, at], key[:, at], (((1,), (1,)), ((), ())), preferred_element_type=jnp.float32
+        ) * (1.0 / math.sqrt(HEAD))
+        weight = jnp.exp(scores - jnp.max(scores, axis=1, keepdims=True))
+        probs = (weight / jnp.sum(weight, axis=1, keepdims=True)).astype(jnp.bfloat16)
+        context.append(jnp.dot(probs, value[:, at], preferred_element_type=jnp.float32))
+    context = jnp.concatenate(context, axis=1).astype(jnp.bfloat16)
+    mixed = dense(context, quarters[3]) + x.astype(jnp.float32)
+    return layer_norm(mixed, gain, bias).astype(jnp.bfloat16)
+
+
+def step_kernel(
+    deep,
+    ids_ref,
+    table_ref,
+    qkv_ref,
+    out_w_ref,
+    gain_ref,
+    bias_ref,
+    cent_ref,
+    assign_ref,
+    loss_ref,
+    new_ref,
+    rows,
+    w,
+    from_y,
+    joined_y,
+    from_z,
+    cent,
+    old,
+    mine,
+    tokens,
+    counts,
+    stat,
+    got,
+    load_sems,
+    send_sems,
+    y_sems,
+    z_sems,
+    w_sems,
+    cent_sems,
+    token_sems,
+    stat_send,
+    stat_recv,
+):
+    place = Place(deep)
+    x, c, z, y = place.x, place.c, place.z, place.y
+    own = place.fsdp
+    parts = 2 * deep
+    vocab_rows, width = table_ref.shape
+    own_rows = mine.shape[0]
+    per_dev = new_ref.shape[0]
+    blocks = 4 * parts
+    own_block = place.dp * parts + own
+    quarter, across = x * 2 + c, (1 - x) * 2 + c
+    partner, x_side, y_side = place.at(c=1 - c), place.at(x=1 - x), place.at(y=1 - y)
+    up, down = place.at(z=jnp.minimum(z + 1, deep - 1)), place.at(z=jnp.maximum(z - 1, 0))
+
+    loads = []
+    for q in range(4):
+        part = qkv_ref.at[:, pl.ds(q * width, width)] if q < 3 else out_w_ref
+        loads.append(pltpu.make_async_copy(part, w.at[q, own], load_sems.at[q]))
+    loads.append(
+        pltpu.make_async_copy(
+            cent_ref.at[:, pl.ds(pl.multiple_of(own * per_dev, 128), per_dev)], cent.at[own], load_sems.at[4]
+        )
+    )
+    for load in loads:
+        load.start()
+
+    def look(block):
+        local = ids_ref[block] - own * vocab_rows
+        hot = local == lax.broadcasted_iota(jnp.int32, (own_rows, vocab_rows), 1)
+        rows[block] = jnp.dot(
+            jnp.where(hot, 1.0, 0.0).astype(jnp.bfloat16), table_ref[...], preferred_element_type=jnp.float32
+        ).astype(jnp.bfloat16)
+
+    look((z + 1) % deep * 2 + (1 - y))
+    place.greet()
+    out = Sender(send_sems)
+    for load in loads:
+        load.wait()
+
+    home = w.at[quarter, own]
+    out.send(home, home, w_sems.at[quarter, own], up, z + 1 < deep)
+    out.send(home, home, w_sems.at[quarter, own], down, z > 0)
+    for k in range(1, deep + 1):
+        to = (z + k) % deep
+        if k > 1:
+            look(to * 2 + (1 - y))
+        out.send(rows.at[to * 2 + (1 - y)], from_y.at[to], y_sems.at[to], y_side)
+    for k in range(1, deep + 1):
+        look((z + k) % deep * 2 + y)
+
+    def spread(s):
+        block = w.at[quarter, s]
+        out.send(block, block, w_sems.at[quarter, s], x_side)
+        out.send(block, block, w_sems.at[quarter, s], partner)
+
+    def join(k):
+        to = (z + k) % deep
+        out.arrived(from_y.at[to], y_sems.at[to], y_side)
+        joined_y[to] = from_y[to] + rows[to * 2 + y]
+        if k < deep:
+            out.send(joined_y.at[to], from_z.at[deep - k], z_sems.at[deep - k], place.at(z=to))
+
+    for k in range(1, deep):
+        z0 = near_first(z, k, deep)
+        s = z0 * 2 + y
+        block = w.at[quarter, s]
+        out.arrived(block, w_sems.at[quarter, s], y_side)
+        out.send(block, block, w_sems.at[quarter, s], up, (z0 < z) & (z + 1 < deep))
+        out.send(block, block, w_sems.at[quarter, s], down, (z0 > z) & (z > 0))
+        spread(s)
+        join(k)
+    join(deep)
+    for k in range(deep):
+        block = w.at[quarter, near_first(z, k, deep) * 2 + y]
+        out.send(block, block, w_sems.at[quarter, near_first(z, k, deep) * 2 + y], y_side)
+    for k in range(1, parts):
+        to = (own + k) % parts
+        columns = pl.ds(pl.multiple_of(to * per_dev, 128), per_dev)
+        out.send(
+            cent_ref.at[:, columns], cent.at[own], cent_sems.at[own], {"dp": place.dp, "fsdp": to}
+        )
+    for k in range(deep):
+        s = near_first(z, k, deep) * 2 + (1 - y)
+        out.arrived(w.at[quarter, s], w_sems.at[quarter, s], y_side)
+        spread(s)
+    others = [near_first(z, k, deep) * 2 + y for k in range(1, deep)]
+    others += [near_first(z, k, deep) * 2 + (1 - y) for k in range(deep)]
+    for s in others:
+        block = w.at[across, s]
+        out.arrived(block, w_sems.at[across, s], x_side)
+        out.send(block, block, w_sems.at[across, s], partner)
+    total = joined_y[z]
+    for k in range(1, deep):
+        out.arrived(from_z.at[k], z_sems.at[k], y_side)
+        total = total + from_z[k]
+    for q in (x * 2 + (1 - c), (1 - x) * 2 + (1 - c)):
+        for s in others:
+            out.arrived(w.at[q, s], w_sems.at[q, s], partner)
+    for first in range(0, own_rows, SEQ):
+        mine[pl.ds(first, SEQ), :] = passage(
+            total[first : first + SEQ], range(4), gain_ref[...], bias_ref[...], w
+        )
+
+    x_first = c == 1
+    second_xy = (jnp.where(x_first, 1 - x, x), jnp.where(x_first, y, 1 - y))
+    third_xy = (jnp.where(x_first, x, 1 - x), jnp.where(x_first, 1 - y, y))
+    second = place.at(x=second_xy[0], y=second_xy[1])
+    third = place.at(x=third_xy[0], y=third_xy[1])
+
+    def number(x0, c0, z0, y0):
+        return ((x0 * 2 + c0) * deep + z0) * 2 + y0
+
+    def push(b, peer, when=None, src=None):
+        block = tokens.at[b]
+        out.send(block if src is None else src, block, token_sems.at[b], peer, when)
+
+    def wait(b):
+        out.arrived(tokens.at[b], token_sems.at[b], partner)
+
+    push(own_block, up, z + 1 < deep, mine)
+    push(own_block, down, z > 0, mine)
+    for peer in (second, third, partner):
+        push(own_block, peer, None, mine)
+    tokens[own_block] = mine[...]
+    new_ref[...] = jnp.zeros_like(new_ref)
+    counts[...] = jnp.zeros_like(counts)
+    base = own_block * per_dev
+    centroid = lax.broadcasted_iota(jnp.int32, (per_dev, 2 * own_rows), 0) + base
+
+    def pair_of(p):
+        hits = centroid == assign_ref[p]
+        return hits, tokens[pl.ds(p * 2, 2)].reshape(2 * own_rows, width)
+
+    def add_up(p):
+        hits, some = pair_of(p)
+        ones = jnp.where(hits, 1.0, 0.0)
+        counts[...] += jnp.sum(ones, axis=1, keepdims=True)
+        new_ref[...] += jnp.dot(
+            ones.astype(jnp.bfloat16), some, preferred_element_type=jnp.float32
+        )
+
+    def score(p):
+        hits, some = pair_of(p)
+        logits = lax.dot_general(
+            old[...], some, (((1,), (1,)), ((), ())), preferred_element_type=jnp.float32
+        )
+        peak = jnp.max(logits, axis=0, keepdims=True)
+        mass = jnp.sum(jnp.exp(logits - peak), axis=0, keepdims=True)
+        pick = jnp.sum(jnp.where(hits, logits, 0.0), axis=0, keepdims=True)
+        for half in range(2):
+            b = p * 2 + half
+            at = slice(half * own_rows, (half + 1) * own_rows)
+            for k, row in enumerate((peak, mass, pick)):
+                stat[b, pl.ds(k, 1), :] = row[:, at]
+            pl.when(b != own_block)(stat_copy(b).start)
+
+    def stat_copy(b):
+        return pltpu.make_async_remote_copy(
+            src_ref=stat.at[b],
+            dst_ref=got.at[own_block],
+            send_sem=stat_send.at[b],
+            recv_sem=stat_recv.at[own_block],
+            device_id={"dp": b // parts, "fsdp": b % parts},
+            device_id_type=pl.DeviceIdType.MESH,
+        )
+
+    def finish_line(z1):
+        for xx, yy in (third_xy, (1 - x, 1 - y)):
+            b = number(xx, c, z1, yy)
+            wait(b)
+            push(b, partner)
+
+    def sums_of(z1):
+        for x0 in range(2):
+            for y0 in range(2):
+                wait(number(x0, 1 - c, z1, y0))
+
+        @pl.loop(0, 4)
+        def each(i):
+            add_up(i * deep + z1)
+
+    for k in range(deep):
+        z0 = near_first(z, k, deep)
+        if k > 0:
+            b = number(x, c, z0, y)
+            wait(b)
+            push(b, up, (z0 < z) & (z + 1 < deep))
+            push(b, down, (z0 > z) & (z > 0))
+            push(b, second)
+            push(b, third)
+            push(b, partner)
+        b = number(second_xy[0], c, z0, second_xy[1])
+        wait(b)
+        push(b, third)
+        push(b, partner)
+        if k >= 1:
+            finish_line(near_first(z, k - 1, deep))
+        if k >= 2:
+            sums_of(near_first(z, k - 2, deep))
+    finish_line(near_first(z, deep - 1, deep))
+    for k in range(1, parts):
+        s = (own + k) % parts
+        out.arrived(cent.at[s], cent_sems.at[s], partner)
+    old[...] = cent[...].reshape(width, per_dev).T
+    for k in range(max(deep - 2, 0), deep):
+        sums_of(near_first(z, k, deep))
+
+    @pl.loop(0, 4 * deep)
+    def each(p):
+        score(p)
+
+    many = counts[...]
+    new_ref[...] = jnp.where(
+        many > 0, new_ref[...] / jnp.maximum(many, 1.0), old[...].astype(jnp.float32)
+    )
+    got[own_block] = stat[own_block]
+
+    @pl.loop(0, blocks)
+    def each_device(b):
+        @pl.when(b != own_block)
+        def done():
+            stat_copy(b).wait_send()
+            pltpu.make_async_remote_copy(
+                src_ref=got.at[b],
+                dst_ref=got.at[b],
+                send_sem=stat_send.at[b],
+                recv_sem=stat_recv.at[b],
+                device_id=partner,
+                device_id_type=pl.DeviceIdType.MESH,
+            ).wait_recv()
+
+    peaks, masses, picks = (got[:, k, :] for k in range(3))
+    top = jnp.max(peaks, axis=0, keepdims=True)
+    mass = jnp.sum(masses * jnp.exp(peaks - top), axis=0, keepdims=True)
+    loss_ref[...] = jnp.log(mass) + top - jnp.sum(picks, axis=0, keepdims=True)
+    out.drain()
+
+
+def token_shards(token_ids, embed_table, w_qkv, w_out, ln_gain, ln_bias, centroids_t, assignments):
+    parts = lax.axis_size("fsdp")
+    deep = parts // 2
+    blocks = 4 * parts
+    width = embed_table.shape[1]
+    feats = w_qkv.shape[0]
+    own_rows = token_ids.shape[0] // parts
+    per_dev = centroids_t.shape[1] // parts
+    half = jnp.bfloat16
+    block = (own_rows, width)
+    sems = pltpu.SemaphoreType.DMA
+    loss, new = pl.pallas_call(
+        functools.partial(step_kernel, deep),
+        out_shape=(
+            jax.ShapeDtypeStruct((1, own_rows), jnp.float32),
+            jax.ShapeDtypeStruct((per_dev, width), jnp.float32),
+        ),
+        in_specs=[
+            WHOLE_VMEM,
+            WHOLE_VMEM,
+            WHOLE_VMEM,
+            WHOLE_VMEM,
+            WHOLE_VMEM,
+            WHOLE_VMEM,
+            pl.BlockSpec(memory_space=pl.ANY),
+            WHOLE_VMEM,
+        ],
+        out_specs=(WHOLE_VMEM, WHOLE_VMEM),
+        scratch_shapes=[
+            pltpu.VMEM((parts, *block), half),
+            pltpu.VMEM((4, parts, feats, width), half),
+            pltpu.VMEM((deep, *block), half),
+            pltpu.VMEM((deep, *block), half),
+            pltpu.VMEM((deep, *block), half),
+            pltpu.VMEM((parts, feats, per_dev), half),
+            pltpu.VMEM((per_dev, width), half),
+            pltpu.VMEM(block, half),
+            pltpu.VMEM((blocks, *block), half),
+            pltpu.VMEM((per_dev, 1), jnp.float32),
+            pltpu.VMEM((blocks, 8, own_rows), jnp.float32),
+            pltpu.VMEM((blocks, 8, own_rows), jnp.float32),
+            sems((5,)),
+            sems((64 * deep,)),
+            sems((deep,)),
+            sems((deep,)),
+            sems((4, parts)),
+            sems((parts,)),
+            sems((blocks,)),
+            sems((blocks,)),
+            sems((blocks,)),
+        ],
+        compiler_params=pltpu.CompilerParams(
+            collective_id=0, has_side_effects=True, vmem_limit_bytes=VMEM_LIMIT
+        ),
+        name="whole_step",
+    )(
+        token_ids.reshape(parts, own_rows, 1),
+        embed_table,
+        w_qkv,
+        w_out,
+        ln_gain[None],
+        ln_bias[None],
+        centroids_t,
+        assignments.reshape(blocks // 2, 1, 2 * own_rows),
+    )
+    return loss.reshape(own_rows), new
+
+
+def plan(mesh):
+    dp_size, fsdp_size = mesh.shape["dp"], mesh.shape["fsdp"]
+
+    def either(*args):
+        few_tokens = args[7].shape[0] <= args[6].shape[1]
+        paired = dp_size == 4 and fsdp_size % 2 == 0
+        return token_shards(*args) if few_tokens and paired else shards(*args)
+
+    return either
+
+
 def solution(mesh):
     return jax.shard_map(
-        shards,
+        plan(mesh),
         mesh=mesh,
         in_specs=(
             P("dp"),

time: 483 us -> 149 us (0.31)
  waiting for transfers between devices: 313 us -> 0 us
  Pallas kernels: 0 us -> 139 us
  matrix products: 78.1 us -> 0 us
  blocking collectives: 34 us -> 0 us
  other arithmetic: 17.9 us -> 0 us
  between operations: 14 us -> 0.64 us
  local copies, waits for them, and re-layouts: 17.3 us -> 9.13 us
  starting transfers between devices: 8.02 us -> 0 us
    all_gather x3 -> x0, waiting for transfers between devices: 237 us -> none  [the longest x1 139 us: shards(): lax.all_gather(centroids_t, 'fsdp', axis=0, tiled=True)]
    pallas_call x0 -> x1, Pallas kernels: none -> 139 us  [token_shards(): pl.pallas_call(functools.partial(step_kernel, deep), out_shape=(jax.Shape...]
    dot_general x13 -> x0, matrix products: 76.6 us -> none  [the longest x8 58.1 us: one_visit(): lax.dot_general(hits, block_rows, (((0,), (0,)), ((), ())), preferred_ele...]
    reduce_scatter x1 -> x0, waiting for transfers between devices: 66.3 us -> none  [shards(): lax.psum_scatter(looked, 'fsdp', scatter_dimension=0, tiled=True)]
    all_gather x5 -> x0, blocking collectives: 34 us -> none  [the longest x3 15.7 us: joined(): everything = jax.tree.map(lambda part: lax.all_gather(part, axis), shard)]
    all_to_all x2 -> x0, starting transfers between devices: 7.87 us -> none  [the longest x1 4.48 us: shards(): lax.all_to_all(partial_share, 'fsdp', split_axis=0, concat_axis=1, tiled=...]
    reduce_sum x3 -> x0, other arithmetic: 7.78 us -> none  [the longest x1 5.64 us: body_visit(): picked = jnp.sum(jnp.where(hits, logits, 0.0), axis=1)]
    all_to_all x2 -> x0, waiting for transfers between devices: 7.77 us -> none  [the longest x1 7.77 us: shards(): lax.all_to_all(encoded, 'fsdp', split_axis=1, concat_axis=0, tiled=True)]
  transfers between devices with their start and end apart: 6 -> 0, of which waited for: 5 -> 0; matrix products, arithmetic and copies ran while one was open for 20% -> 0% of each run, Pallas kernels for 0% -> 0%
where the time goes in v2:
time: 149 us
  Pallas kernels  139 us (93%)
  local copies, waits for them, and re-layouts  9.13 us (6%)
    pallas_call x1, Pallas kernels, token_shards(): pl.pallas_call(functools.partial(step_kernel, deep), out_shape=(jax.Shape...  139 us
    unnamed x2, local copies, waits for them, and re-layouts  4.87 us

profile of v2, /device:TPU:0, one launch (start us, length us, event | category | flops | bytes accessed | tf_op | source)
XLA Modules:
  0.0 148.9 jit_solution(625813910394243568)
XLA Ops:
  0.6 1.3 broadcast_in_dim.6.gain_ref
  1.9 1.3 broadcast_in_dim.7.bias_ref
  3.2 1.7 %copy.10.ids_ref = s32[8,128,1]{2,1,0:T(8,128)} copy(s32[8,128,1]{1,0,2:T(8,128)} %bitcast.4) | data formatting | bytes 8192 | tf_op jit(solution)/shard_map/reshape | solution.py:586
  4.9 139.1 %whole_step.1 = (f32[1,128]{1,0:T(1,128)}, f32[1024,768]{1,0:T(8,128)}) custom-call(s32[8,128,1]{2,1,0:T(8,128)} %copy.10.ids_ref, bf16[1908,768]{1,0:T(8,128)(2,1)} %table_ref.1, bf16[96,2304]{1,0:T(8,128)(2,1)} %qkv_ref.1, bf16[96,768]{1,0:T(8,128)(2,1)} %out_w_ref.1, f32[1,768]{1,0:T(1,128)} %broadcast_in_dim.6.gain_ref, ...), custom_call_target="tpu_custom_call" | custom-call | tf_op jit(solution)/shard_map/whole_step/pallas_call | solution.py:541
  144.0 1.1 copy.13
  145.2 3.8 %copy.14 = f32[1024,768]{1,0:T(8,128)} copy(f32[1024,768]{1,0:T(8,128)} %get-tuple-element.9) | data formatting | bytes 6291456

commit v3 on v2

--- a/solution.py
+++ b/solution.py
@@ -262,8 +262,7 @@
     table_ref,
     qkv_ref,
     out_w_ref,
-    gain_ref,
-    bias_ref,
+    norm_ref,
     cent_ref,
     assign_ref,
     loss_ref,
@@ -315,14 +314,14 @@
     for load in loads:
         load.start()
 
-    def look(block):
-        local = ids_ref[block] - own * vocab_rows
-        hot = local == lax.broadcasted_iota(jnp.int32, (own_rows, vocab_rows), 1)
-        rows[block] = jnp.dot(
+    def look(y0):
+        local = ids_ref[y0] - own * vocab_rows
+        hot = local == lax.broadcasted_iota(jnp.int32, (deep * own_rows, vocab_rows), 1)
+        found = jnp.dot(
             jnp.where(hot, 1.0, 0.0).astype(jnp.bfloat16), table_ref[...], preferred_element_type=jnp.float32
-        ).astype(jnp.bfloat16)
-
-    look((z + 1) % deep * 2 + (1 - y))
+        )
+        rows[y0] = found.astype(jnp.bfloat16).reshape(deep, own_rows, width)
+
     place.greet()
     out = Sender(send_sems)
     for load in loads:
@@ -333,11 +332,10 @@
     out.send(home, home, w_sems.at[quarter, own], down, z > 0)
     for k in range(1, deep + 1):
         to = (z + k) % deep
-        if k > 1:
-            look(to * 2 + (1 - y))
-        out.send(rows.at[to * 2 + (1 - y)], from_y.at[to], y_sems.at[to], y_side)
-    for k in range(1, deep + 1):
-        look((z + k) % deep * 2 + y)
+        if k == 1:
+            look(1 - y)
+        out.send(rows.at[1 - y, to], from_y.at[to], y_sems.at[to], y_side)
+    look(y)
 
     def spread(s):
         block = w.at[quarter, s]
@@ -347,7 +345,7 @@
     def join(k):
         to = (z + k) % deep
         out.arrived(from_y.at[to], y_sems.at[to], y_side)
-        joined_y[to] = from_y[to] + rows[to * 2 + y]
+        joined_y[to] = from_y[to] + rows[y, to]
         if k < deep:
             out.send(joined_y.at[to], from_z.at[deep - k], z_sems.at[deep - k], place.at(z=to))
 
@@ -359,21 +357,27 @@
         out.send(block, block, w_sems.at[quarter, s], up, (z0 < z) & (z + 1 < deep))
         out.send(block, block, w_sems.at[quarter, s], down, (z0 > z) & (z > 0))
         spread(s)
+    for k in range(1, deep + 1):
         join(k)
-    join(deep)
     for k in range(deep):
         block = w.at[quarter, near_first(z, k, deep) * 2 + y]
         out.send(block, block, w_sems.at[quarter, near_first(z, k, deep) * 2 + y], y_side)
-    for k in range(1, parts):
-        to = (own + k) % parts
+
+    def give(z0, y0):
+        to = z0 * 2 + y0
         columns = pl.ds(pl.multiple_of(to * per_dev, 128), per_dev)
         out.send(
             cent_ref.at[:, columns], cent.at[own], cent_sems.at[own], {"dp": place.dp, "fsdp": to}
         )
+
+    for k in range(1, deep):
+        give((z + k) % deep, y)
     for k in range(deep):
         s = near_first(z, k, deep) * 2 + (1 - y)
         out.arrived(w.at[quarter, s], w_sems.at[quarter, s], y_side)
         spread(s)
+    for k in range(deep):
+        give((z + k) % deep, 1 - y)
     others = [near_first(z, k, deep) * 2 + y for k in range(1, deep)]
     others += [near_first(z, k, deep) * 2 + (1 - y) for k in range(deep)]
     for s in others:
@@ -389,7 +393,7 @@
             out.arrived(w.at[q, s], w_sems.at[q, s], partner)
     for first in range(0, own_rows, SEQ):
         mine[pl.ds(first, SEQ), :] = passage(
-            total[first : first + SEQ], range(4), gain_ref[...], bias_ref[...], w
+            total[first : first + SEQ], range(4), norm_ref[0:1, :], norm_ref[1:2, :], w
         )
 
     x_first = c == 1
@@ -455,13 +459,19 @@
             device_id_type=pl.DeviceIdType.MESH,
         )
 
+    def take_centroids():
+        for k in range(1, parts):
+            s = (own + k) % parts
+            out.arrived(cent.at[s], cent_sems.at[s], partner)
+        old[...] = cent[...].reshape(width, per_dev).T
+
     def finish_line(z1):
         for xx, yy in (third_xy, (1 - x, 1 - y)):
             b = number(xx, c, z1, yy)
             wait(b)
             push(b, partner)
 
-    def sums_of(z1):
+    def sums_of(z1, with_scores):
         for x0 in range(2):
             for y0 in range(2):
                 wait(number(x0, 1 - c, z1, y0))
@@ -469,6 +479,8 @@
         @pl.loop(0, 4)
         def each(i):
             add_up(i * deep + z1)
+            if with_scores:
+                score(i * deep + z1)
 
     for k in range(deep):
         z0 = near_first(z, k, deep)
@@ -486,19 +498,13 @@
         push(b, partner)
         if k >= 1:
             finish_line(near_first(z, k - 1, deep))
+        if k == deep - 2:
+            take_centroids()
         if k >= 2:
-            sums_of(near_first(z, k - 2, deep))
+            sums_of(near_first(z, k - 2, deep), True)
     finish_line(near_first(z, deep - 1, deep))
-    for k in range(1, parts):
-        s = (own + k) % parts
-        out.arrived(cent.at[s], cent_sems.at[s], partner)
-    old[...] = cent[...].reshape(width, per_dev).T
-    for k in range(max(deep - 2, 0), deep):
-        sums_of(near_first(z, k, deep))
-
-    @pl.loop(0, 4 * deep)
-    def each(p):
-        score(p)
+    for k in range(deep - 2, deep):
+        sums_of(near_first(z, k, deep), True)
 
     many = counts[...]
     new_ref[...] = jnp.where(
@@ -550,13 +556,12 @@
             WHOLE_VMEM,
             WHOLE_VMEM,
             WHOLE_VMEM,
-            WHOLE_VMEM,
             pl.BlockSpec(memory_space=pl.ANY),
             WHOLE_VMEM,
         ],
         out_specs=(WHOLE_VMEM, WHOLE_VMEM),
         scratch_shapes=[
-            pltpu.VMEM((parts, *block), half),
+            pltpu.VMEM((2, deep, *block), half),
             pltpu.VMEM((4, parts, feats, width), half),
             pltpu.VMEM((deep, *block), half),
             pltpu.VMEM((deep, *block), half),
@@ -583,12 +588,11 @@
         ),
         name="whole_step",
     )(
-        token_ids.reshape(parts, own_rows, 1),
+        token_ids.reshape(deep, 2, own_rows).transpose(1, 0, 2).reshape(2, deep * own_rows, 1),
         embed_table,
         w_qkv,
         w_out,
-        ln_gain[None],
-        ln_bias[None],
+        jnp.stack([ln_gain, ln_bias]),
         centroids_t,
         assignments.reshape(blocks // 2, 1, 2 * own_rows),
     )

time: 149 us -> 138 us (0.926); the launches traced: 149 us -> 136 us
  Pallas kernels: 139 us -> 127 us
    pallas_call x1, Pallas kernels: 139 us -> 127 us  [token_shards(): pl.pallas_call(functools.partial(step_kernel, deep), out_shape=(jax.Shape...]
    broadcast_in_dim x2 -> x0, local copies, waits for them, and re-layouts: 2.55 us -> none  [the longest x1 1.28 us: token_shards(): ln_bias[None]]
where the time goes in v3:
time: 138 us; the launch traced here: 136 us
  Pallas kernels  127 us (92%)
  local copies, waits for them, and re-layouts  8.03 us (6%)
    pallas_call x1, Pallas kernels, token_shards(): pl.pallas_call(functools.partial(step_kernel, deep), out_shape=(jax.Shape...  127 us
    unnamed x2, local copies, waits for them, and re-layouts  4.95 us

profile of v3, /device:TPU:0, one launch (start us, length us, event | category | flops | bytes accessed | tf_op | source)
XLA Modules:
  0.0 136.3 jit_solution(10549215433164825752)
XLA Ops:
  0.6 0.7 stack.9
  1.3 0.7 stack.10
  2.0 0.6 pad_maximum_fusion.norm_ref
  2.6 1.7 %copy.10.ids_ref = s32[2,512,1]{2,1,0:T(8,128)} copy(s32[2,512,1]{1,0,2:T(2,128)} %bitcast.8) | data formatting | bytes 8192 | tf_op jit(solution)/shard_map/reshape | solution.py:591
  4.3 127.1 %whole_step.1 = (f32[1,128]{1,0:T(1,128)}, f32[1024,768]{1,0:T(8,128)}) custom-call(s32[2,512,1]{2,1,0:T(8,128)} %copy.10.ids_ref, bf16[1908,768]{1,0:T(8,128)(2,1)} %table_ref.1, bf16[96,2304]{1,0:T(8,128)(2,1)} %qkv_ref.1, bf16[96,768]{1,0:T(8,128)(2,1)} %out_w_ref.1, f32[2,768]{1,0:T(2,128)} %pad_maximum_fusion.norm_ref, bf16[96,8192]{1,0:T(8,128)(2,1)} %cent_ref.1, ...), custom_call_target="tpu_custom_call" | custom-call | tf_op jit(solution)/shard_map/whole_step/pallas_call | solution.py:547
  131.4 1.2 copy.13
  132.6 3.8 %copy.14 = f32[1024,768]{1,0:T(8,128)} copy(f32[1024,768]{1,0:T(8,128)} %get-tuple-element.9) | data formatting | bytes 6291456

commit v4 on v3

--- a/solution.py
+++ b/solution.py
@@ -502,9 +502,9 @@
             take_centroids()
         if k >= 2:
             sums_of(near_first(z, k - 2, deep), True)
+    sums_of(near_first(z, deep - 2, deep), True)
     finish_line(near_first(z, deep - 1, deep))
-    for k in range(deep - 2, deep):
-        sums_of(near_first(z, k, deep), True)
+    sums_of(near_first(z, deep - 1, deep), True)
 
     many = counts[...]
     new_ref[...] = jnp.where(

time: 138 us -> 139 us (level)
  no operation moved by 1% of the time
where the time goes in v4:
time: 139 us; the launch traced here: 137 us
  Pallas kernels  128 us (92%)
  local copies, waits for them, and re-layouts  8.03 us (6%)
    pallas_call x1, Pallas kernels, token_shards(): pl.pallas_call(functools.partial(step_kernel, deep), out_shape=(jax.Shape...  128 us
    unnamed x2, local copies, waits for them, and re-layouts  4.95 us

profile of v4, /device:TPU:0, one launch (start us, length us, event | category | flops | bytes accessed | tf_op | source)
XLA Modules:
  0.0 137.3 jit_solution(6249733409753639607)
XLA Ops:
  0.6 0.7 stack.9
  1.3 0.7 stack.10
  2.0 0.6 pad_maximum_fusion.norm_ref
  2.6 1.7 %copy.10.ids_ref = s32[2,512,1]{2,1,0:T(8,128)} copy(s32[2,512,1]{1,0,2:T(2,128)} %bitcast.8) | data formatting | bytes 8192 | tf_op jit(solution)/shard_map/reshape | solution.py:591
  4.3 128.0 %whole_step.1 = (f32[1,128]{1,0:T(1,128)}, f32[1024,768]{1,0:T(8,128)}) custom-call(s32[2,512,1]{2,1,0:T(8,128)} %copy.10.ids_ref, bf16[1908,768]{1,0:T(8,128)(2,1)} %table_ref.1, bf16[96,2304]{1,0:T(8,128)(2,1)} %qkv_ref.1, bf16[96,768]{1,0:T(8,128)(2,1)} %out_w_ref.1, f32[2,768]{1,0:T(2,128)} %pad_maximum_fusion.norm_ref, bf16[96,8192]{1,0:T(8,128)(2,1)} %cent_ref.1, ...), custom_call_target="tpu_custom_call" | custom-call | tf_op jit(solution)/shard_map/whole_step/pallas_call | solution.py:547
  132.3 1.2 copy.13
  133.5 3.8 %copy.14 = f32[1024,768]{1,0:T(8,128)} copy(f32[1024,768]{1,0:T(8,128)} %get-tuple-element.9) | data formatting | bytes 6291456
